TPU v7x, 32 devices: a whole 2x2x4 slice. The times are simulated.
32 devices in a mesh: groups: 2 (over y), state: 4 (over z), type: 4 (over x, core).
Axes of the slice: x: 2, y: 2, z: 4, core: 2. Of those that a mesh axis runs over, the one named last changes fastest.
Arguments:
- value_in: bfloat16 [16384, 2048], P(('groups', 'state'), 'type'), parts along dimension 0, may hold values from -7.5 to 7.5
- cotangent: bfloat16 [16384, 2048], P(('groups', 'state'), 'type'), parts along dimension 0, may hold values from -100 to 100
- state_util: float32 [2, 16384], P(None, ('groups', 'state')), parts along dimension 1, may hold values from -300 to 300
- taste: float32 [2, 4096], P(None, ('groups', 'type')), parts along dimension 1, may hold values from -6 to 6
- tiles: bfloat16 [128, 2, 6, 128, 128], P(('groups', 'state')), parts along dimension 0, may hold values from 0 to 0.0051879883
- dest_block: int32 [128, 2, 6], P(('groups', 'state')), parts along dimension 0, may hold values from 0 to 63, as said below
- counts: int32 [128, 2], P(('groups', 'state')), parts along dimension 0, may hold values from 1 to 6
Outputs:
- value_out: float32 [16384, 2048], P(('groups', 'state'), 'type'), parts along dimension 0
- adjoint: float32 [16384, 2048], P(('groups', 'state'), 'type'), parts along dimension 0
- grad_util: float32 [2, 16384], P(None, ('groups', 'state')), parts along dimension 1
- grad_taste: float32 [2, 4096], P(None, ('groups', 'type')), parts along dimension 1
There are 2 independent parts, one for each index of `groups`. A program takes and returns all parts, laid end to end along the dimension named above; each array names one. Nothing has to cross between parts.
Inputs may be any that keep to these rules, and one draw needn't show every extreme that they name: `dest_block`: entries at or beyond a list's count name blocks of the list's own run of 16 blocks. In each run of 16 blocks exactly 16 used entries name blocks outside the run, at most 6 of them in any one other run, and exactly 6 in some other run.
All inputs are finite; a program needn't handle non-finite values.
Results may differ from a plain program's by a relative error of at most 0.0012.
Values may be sent and summed in bfloat16 or wider, within the bound.
A program may use at most 192 MiB of HBM per device.

v0:
```python
import functools

import jax
import jax.numpy as jnp
from jax import lax
from jax.experimental import pallas as pl
from jax.experimental.pallas import tpu as pltpu
from jax.sharding import PartitionSpec as P

VMEM = pltpu.VMEM
SMEM = pltpu.SMEM
MESH = pl.DeviceIdType.MESH


def smem():
    return pl.BlockSpec(memory_space=SMEM)


def whole(shape):
    return pl.BlockSpec(shape, lambda *g: (0,) * len(shape))


def plan_kernel(dims, me_ref, dest_ref, count_ref, req_ref, look_ref, from_ref, fill):
    B, A, M, D, cap = dims
    me = me_ref[0]

    def clear(p, carry):
        fill[p] = 0
        for s in range(cap):
            req_ref[p, 0, s] = -1
            from_ref[p * cap + s] = 0
        return carry

    lax.fori_loop(0, D, clear, 0)

    def lists(i, carry):
        for a in range(A):
            count = count_ref[a, i]
            for n in range(M):
                e = (i * A + a) * M + n
                dest = dest_ref[n, a, i]
                owner = lax.div(dest, B)
                block = dest - owner * B
                used = n < count
                look_ref[e] = jnp.where(used & (owner == me), block, -1)

                @pl.when(used & (owner != me))
                def _():
                    s = fill[owner]
                    fill[owner] = s + 1
                    req_ref[owner, 0, s] = block
                    from_ref[owner * cap + s] = e
                    look_ref[e] = B + owner * cap + s

        return carry

    lax.fori_loop(0, B, lists, 0)


def greet(axis, others):
    barrier = pltpu.get_barrier_semaphore()
    for ids in others:
        pl.semaphore_signal(barrier, inc=1, device_id=ids, device_id_type=MESH)
    pl.semaphore_wait(barrier, len(others))


def request_kernel(D, req_ref, out_ref, land, send, recv):
    me = lax.axis_index("state")
    peers = [{"state": lax.rem(me + k, D)} for k in range(1, D)]
    greet("state", peers)
    copies = []
    for k in range(1, D):
        c = pltpu.make_async_remote_copy(
            src_ref=req_ref.at[lax.rem(me + k, D)],
            dst_ref=land.at[k],
            send_sem=send.at[k],
            recv_sem=recv.at[k],
            device_id={"state": lax.rem(me + k, D)},
            device_id_type=MESH,
        )
        c.start()
        copies.append(c)
    for c in copies:
        c.wait()
    out_ref[me] = req_ref[me]
    for k in range(1, D):
        out_ref[lax.rem(me - k + D, D)] = land[k]


def gather_kernel(D, cap, half, want_ref, val_ref, *rest):
    outs, sem = rest[:-1], rest[-1]

    def run(h, act):
        def peer(p, carry):
            for s in range(cap):
                w = jnp.maximum(want_ref[p, 0, s], 0)
                act(
                    pltpu.make_async_copy(
                        val_ref.at[w, :, pl.ds(h * half, half)],
                        outs[h].at[p * cap + s],
                        sem.at[h, p * cap + s],
                    )
                )
            return carry

        lax.fori_loop(0, D, peer, 0)

    for h in range(len(outs)):
        run(h, lambda c: c.start())
    for h in range(len(outs)):
        run(h, lambda c: c.wait())


def transposed_dot(tile, right):
    return lax.dot_general(tile, right, (((0,), (0,)), ((), ())), preferred_element_type=jnp.float32)


def continuation(M, first, look_ref, table, tiles):
    weights, values = [], []
    for n in range(M):
        row = look_ref[first + n]
        keep = jnp.where(row >= 0, 1.0, 0.0).astype(jnp.float32)
        tile = tiles(n)
        weights.append(tile * jnp.full(tile.shape, keep, jnp.float32).astype(jnp.bfloat16))
        values.append(table[jnp.maximum(row, 0)])
    return jnp.dot(
        jnp.concatenate(weights, axis=1), jnp.concatenate(values, axis=0), preferred_element_type=jnp.float32
    )


def fetch_value_kernel(G, rows, D, look_ref, from_ref, val_ref, *rest):
    H = (len(rest) - 14) // 2
    outs, rest = rest[:H], rest[H:]
    body, lands = rest[:9], rest[9 : 9 + H - 1]
    acc, table, kept, sem, send, recv = rest[9 + H - 1 :]
    step = pl.program_id(0)
    B, C, V = val_ref.shape[0], outs[0].shape[0], outs[0].shape[2]
    cap = C // D
    me = lax.axis_index("state")

    def copy(h, k):
        to = lax.rem(me + k, D)
        land = table.at[pl.ds(B + me * cap, cap)] if h == 0 else lands[h - 1].at[pl.ds(me * cap, cap)]
        return pltpu.make_async_remote_copy(
            src_ref=outs[h].at[pl.ds(to * cap, cap)],
            dst_ref=land,
            send_sem=send.at[h, k],
            recv_sem=recv.at[h, k],
            device_id={"state": to},
            device_id_type=MESH,
        )

    @pl.when(step == 0)
    def _():
        greet("state", [{"state": lax.rem(me + k, D)} for k in range(1, D)])
        for h in range(H):
            for k in range(1, D):
                copy(h, k).start()
        own = pltpu.make_async_copy(val_ref.at[:, :, pl.ds(0, V)], table.at[pl.ds(0, B)], sem.at[0])
        mine = pltpu.make_async_copy(
            outs[0].at[pl.ds(me * cap, cap)], table.at[pl.ds(B + me * cap, cap)], sem.at[1]
        )
        own.start()
        mine.start()
        own.wait()
        mine.wait()
        for k in range(1, D):
            copy(0, k).wait()

    work(G, rows, look_ref, from_ref, *body, acc, table, kept)

    @pl.when(step == pl.num_programs(0) - 1)
    def _():
        for h in range(1, H):
            for k in range(1, D):
                copy(h, k).wait()


def value_kernel(
    G, rows, col, look_ref, from_ref, val_ref, inc_ref, tiles_ref, cot_ref, util_ref, taste_ref, *rest
):
    before_ref = rest[0]
    value_ref, scaled_ref, out_ref, gu_ref, gt_ref, acc, table, kept, sem = rest[-9:]
    step = pl.program_id(0)
    B, C, V = val_ref.shape[0], inc_ref.shape[0], inc_ref.shape[2]

    @pl.when(step == 0)
    def _():
        own = pltpu.make_async_copy(val_ref.at[:, :, pl.ds(col, V)], table.at[pl.ds(0, B)], sem.at[0])
        far = pltpu.make_async_copy(inc_ref, table.at[pl.ds(B, C)], sem.at[1])
        own.start()
        far.start()
        own.wait()
        far.wait()

    value_ref[:, :col] = before_ref[...]
    work(
        G, rows, look_ref, from_ref, tiles_ref, cot_ref, util_ref, taste_ref,
        value_ref.at[:, col:], scaled_ref, out_ref, gu_ref, gt_ref, acc, table, kept,
    )


def work(
    G, rows, look_ref, from_ref, tiles_ref, cot_ref, util_ref, taste_ref,
    value_ref, scaled_ref, out_ref, gu_ref, gt_ref, acc, table, kept,
):
    step = pl.program_id(0)
    _, A, M, R, _ = tiles_ref.shape
    C = out_ref.shape[0]

    @pl.when(step == 0)
    def _():
        gt_ref[...] = jnp.zeros_like(gt_ref)

    t0, t1 = taste_ref[0:1, :], taste_ref[1:2, :]
    for g in range(G):
        i = step * G + g
        for a in range(A):
            acc[g, a] = continuation(M, (i * A + a) * M, look_ref, table, lambda n: tiles_ref[i, a, n])
    for g in range(G):
        g0 = g1 = 0.0
        cols = [
            jnp.transpose(jnp.broadcast_to(util_ref[a : a + 1, g * R : (g + 1) * R], (R, R))) for a in range(A)
        ]
        for c in range(0, R, rows):
            at = slice(c, c + rows)
            here = slice(g * R + c, g * R + c + rows)
            q0 = cols[0][at, 0:1] + t0 + 0.95 * acc[g, 0, at, :]
            q1 = cols[1][at, 0:1] + t1 + 0.95 * acc[g, 1, at, :]
            gap = q1 - q0
            small = jnp.exp(-jnp.abs(gap))
            total = 1.0 + small
            value_ref[here, :] = jnp.maximum(q0, q1) + jnp.log(total)
            big = cot_ref[here, :].astype(jnp.float32) / total
            little = big * small
            first_wins = gap <= 0.0
            h0 = jnp.where(first_wins, big, little)
            h1 = jnp.where(first_wins, little, big)
            scaled_ref[g, 0, at, :] = (0.95 * h0).astype(jnp.bfloat16)
            scaled_ref[g, 1, at, :] = (0.95 * h1).astype(jnp.bfloat16)
            gu_ref[g, at, 0:1] = jnp.sum(h0, axis=1, keepdims=True)
            gu_ref[g, at, 1:2] = jnp.sum(h1, axis=1, keepdims=True)
            g0, g1 = g0 + h0, g1 + h1
        gt_ref[0:1, :] += jnp.sum(g0, axis=0, keepdims=True)
        gt_ref[1:2, :] += jnp.sum(g1, axis=0, keepdims=True)
    kept[pl.ds(step * G, G)] = scaled_ref[...]

    @pl.when(step == pl.num_programs(0) - 1)
    def _():
        def back(q, carry):
            for u in range(2):
                slot = q * 2 + u
                e = from_ref[slot]
                pair = lax.div(e, M)
                i = lax.div(pair, A)
                a = pair - i * A
                out_ref[slot] = transposed_dot(tiles_ref[i, a, e - pair * M], kept[i, a]).astype(jnp.bfloat16)
            return carry

        lax.fori_loop(0, C // 2, back, 0)


def back_kernel(G, A, M, look_ref, tiles_ref, scaled_ref, adj_ref):
    spare = adj_ref.shape[0] - 1
    step = pl.program_id(0)

    @pl.when(step == 0)
    def _():
        adj_ref[...] = jnp.zeros_like(adj_ref)

    for g in range(G):
        i = step * G + g
        for a in range(A):
            for n in range(M):
                block = look_ref[(i * A + a) * M + n]
                here = jnp.where((block >= 0) & (block < spare), block, spare)
                adj_ref[here] += transposed_dot(tiles_ref[g, a, n], scaled_ref[g, a])


def sums_kernel(D, T, gu_ref, gt_ref, token_ref, after_ref, ou_ref, ot_ref, lu, lt, us, ur, ts, tr):
    ms, mt = lax.axis_index("state"), lax.axis_index("type")
    peers = [{"state": lax.rem(ms + k, D)} for k in range(1, D)]
    peers += [{"type": lax.rem(mt + k, T)} for k in range(1, T)]
    greet("state", peers)
    copies = []
    for k in range(1, T):
        copies.append(
            pltpu.make_async_remote_copy(
                src_ref=gu_ref, dst_ref=lu.at[k], send_sem=us.at[k], recv_sem=ur.at[k],
                device_id={"type": lax.rem(mt + k, T)}, device_id_type=MESH,
            )
        )
    for k in range(1, D):
        copies.append(
            pltpu.make_async_remote_copy(
                src_ref=gt_ref, dst_ref=lt.at[k], send_sem=ts.at[k], recv_sem=tr.at[k],
                device_id={"state": lax.rem(ms + k, D)}, device_id_type=MESH,
            )
        )
    for c in copies:
        c.start()
    for c in copies:
        c.wait()
    lu[0] = gu_ref[...]
    lt[0] = gt_ref[...]
    u = lu[lax.rem(mt, T)]
    for j in range(1, T):
        u = u + lu[lax.rem(mt - j + T, T)]
    t = lt[lax.rem(ms, D)]
    for j in range(1, D):
        t = t + lt[lax.rem(ms - j + D, D)]
    ou_ref[...] = u
    ot_ref[...] = t


def land_kernel(D, cap, want_ref, adj_ref, ret_ref, *rest):
    out_ref, done_ref = rest[-2:]
    done_ref[0] = 0
    out_ref[...] = adj_ref[...]

    def peer(p, carry):
        for s in range(cap):
            w = want_ref[p, 0, s]

            @pl.when(w >= 0)
            def _():
                out_ref[w] += ret_ref[p * cap + s].astype(jnp.float32)

        return carry

    lax.fori_loop(0, D, peer, 0)


def local(value_in, cotangent, state_util, taste, tiles, dest_block, counts):
    B, A, M, R, _ = tiles.shape
    W = value_in.shape[1]
    D = lax.axis_size("state")
    T = lax.axis_size("type")
    cap = max(2, (B + D - 2) // (D - 1))
    E, C = B * A * M, D * cap
    f32, bf16, i32 = jnp.float32, jnp.bfloat16, jnp.int32
    shape = jax.ShapeDtypeStruct
    values = value_in.reshape(B, R, W)

    req, look, origin = pl.pallas_call(
        functools.partial(plan_kernel, (B, A, M, D, cap)),
        out_shape=(shape((D, 1, 128), i32), shape((E,), i32), shape((C,), i32)),
        in_specs=[smem()] * 3,
        out_specs=[smem()] * 3,
        scratch_shapes=[SMEM((D,), i32)],
        name="plan",
    )(lax.axis_index("state").reshape(1).astype(i32), dest_block.transpose(2, 1, 0), counts.T)

    wanted = pl.pallas_call(
        functools.partial(request_kernel, D),
        out_shape=shape((D, 1, 128), i32),
        in_specs=[pl.BlockSpec(memory_space=VMEM)],
        out_specs=pl.BlockSpec(memory_space=VMEM),
        scratch_shapes=[VMEM((D, 1, 128), i32), pltpu.SemaphoreType.DMA((D,)), pltpu.SemaphoreType.DMA((D,))],
        compiler_params=pltpu.CompilerParams(collective_id=0, has_side_effects=True),
        name="request",
    )(req)

    H = 2 if W % 256 == 0 else 1
    V = W // H
    G = 4 if B % 4 == 0 else 1
    outgoing = pl.pallas_call(
        functools.partial(gather_kernel, D, cap, V),
        out_shape=tuple(shape((C, R, V), bf16) for h in range(H)),
        in_specs=[smem(), pl.BlockSpec(memory_space=VMEM)],
        out_specs=[pl.BlockSpec(memory_space=pl.ANY)] * H,
        scratch_shapes=[pltpu.SemaphoreType.DMA((H, C))],
        name="gather",
    )(wanted, values)

    def exchange(x):
        return lax.all_to_all(
            x.reshape(D, cap, R, V), "state", split_axis=0, concat_axis=0, tiled=True
        ).reshape(C, R, V)

    incoming = []

    flops = 2 * E * R * R * W
    value = None
    gus, gts, outbound, scaleds = [], [], [], []
    any_spec = pl.BlockSpec(memory_space=pl.ANY)
    for h in range(H):
        wide = V * (h + 1)
        ins = [
            whole((B, A, M, R, R)),
            pl.BlockSpec((G * R, V), lambda i, h=h: (i, h)),
            pl.BlockSpec((A, G * R), lambda i: (0, i)),
            pl.BlockSpec((A, V), lambda i, h=h: (0, h)),
        ]
        out_shape = [
            shape((B * R, wide), f32), shape((B, A, R, V), bf16), shape((C, R, V), bf16),
            shape((B, R, A), f32), shape((A, V), f32),
        ]
        out_specs = [
            pl.BlockSpec((G * R, wide), lambda i: (i, 0)),
            pl.BlockSpec((G, A, R, V), lambda i: (i, 0, 0, 0)),
            whole((C, R, V)),
            pl.BlockSpec((G, R, A), lambda i: (i, 0, 0)),
            whole((A, V)),
        ]
        scratch = [
            VMEM((G, A, R, V), f32), VMEM((B + C, R, V), bf16), VMEM((B, A, R, V), bf16),
            pltpu.SemaphoreType.DMA((2,)),
        ]
        cost = pl.CostEstimate(flops=flops // H, bytes_accessed=(24 << 20) // H, transcendentals=3 * B * R * V)
        if h == 0:
            value, scaled, out, gu, gt, *incoming = pl.pallas_call(
                functools.partial(fetch_value_kernel, G, 32, D),
                grid=(B // G,),
                out_shape=out_shape + [shape((C, R, V), bf16)] * (H - 1),
                in_specs=[smem(), smem(), any_spec] + [any_spec] * H + ins,
                out_specs=out_specs + [any_spec] * (H - 1),
                scratch_shapes=scratch + [pltpu.SemaphoreType.DMA((H, D)), pltpu.SemaphoreType.DMA((H, D))],
                compiler_params=pltpu.CompilerParams(collective_id=2, has_side_effects=True),
                cost_estimate=cost,
                name="fetch",
            )(look, origin, values, *outgoing, tiles, cotangent, state_util, taste)
        else:
            value, scaled, out, gu, gt = pl.pallas_call(
                functools.partial(value_kernel, G, 32, h * V),
                grid=(B // G,),
                out_shape=out_shape,
                in_specs=[smem(), smem(), any_spec, any_spec] + ins
                + [pl.BlockSpec((G * R, h * V), lambda i: (i, 0))],
                out_specs=out_specs,
                scratch_shapes=scratch,
                cost_estimate=cost,
                name="value",
            )(look, origin, values, incoming[h - 1], tiles, cotangent, state_util, taste, value)
        outbound.append(out)
        scaleds.append(scaled)
        gus.append(gu)
        gts.append(gt)

    adjs = [
        pl.pallas_call(
            functools.partial(back_kernel, G, A, M),
            grid=(B // G,),
            out_shape=shape((B + 1, R, V), f32),
            in_specs=[
                smem(),
                pl.BlockSpec((G, A, M, R, R), lambda i: (i, 0, 0, 0, 0)),
                pl.BlockSpec((G, A, R, V), lambda i: (i, 0, 0, 0)),
            ],
            out_specs=whole((B + 1, R, V)),
            cost_estimate=pl.CostEstimate(flops=flops // H, bytes_accessed=(14 << 20) // H, transcendentals=0),
            name="back",
        )(look, tiles, x)
        for x in scaleds
    ]

    returned = []
    for h in range(H):
        if h > 0:
            outbound[h], adjs[h - 1] = lax.optimization_barrier((outbound[h], adjs[h - 1]))
        returned.append(exchange(outbound[h]))

    adjoint, tokens = None, []
    gu_rows = sum(gus).transpose(2, 0, 1).reshape(A, B * R) / (W * T)
    for h in range(H):
        held = [] if h == 0 else [adjoint]
        adjoint, token = pl.pallas_call(
            functools.partial(land_kernel, D, cap),
            grid=(1,),
            out_shape=(shape((B, R, W), f32), shape((1,), i32)),
            in_specs=[smem(), whole((B, R, V)), whole((C, R, V))]
            + [pl.BlockSpec(memory_space=pl.ANY)] * len(held),
            out_specs=[pl.BlockSpec((B, R, V), lambda j, h=h: (0, 0, h)), smem()],
            input_output_aliases={3 + k: k for k in range(len(held))},
            name="land",
        )(wanted, adjs[h], returned[h], *held)
        tokens.append(token)
    grad_util, grad_taste = pl.pallas_call(
        functools.partial(sums_kernel, D, T),
        out_shape=(shape((A, B * R), f32), shape((A, W), f32)),
        in_specs=[pl.BlockSpec(memory_space=VMEM)] * 2 + [smem(), pl.BlockSpec(memory_space=pl.ANY)],
        out_specs=[pl.BlockSpec(memory_space=VMEM)] * 2,
        scratch_shapes=[
            VMEM((T, A, B * R), f32), VMEM((D, A, W), f32),
            pltpu.SemaphoreType.DMA((T,)), pltpu.SemaphoreType.DMA((T,)),
            pltpu.SemaphoreType.DMA((D,)), pltpu.SemaphoreType.DMA((D,)),
        ],
        compiler_params=pltpu.CompilerParams(collective_id=1, has_side_effects=True),
        cost_estimate=pl.CostEstimate(flops=0, bytes_accessed=8 << 20, transcendentals=0),
        name="sums",
    )(gu_rows, jnp.concatenate(gts, axis=1) / (B * R * D), tokens[0], adjs[-1])

    return value, adjoint.reshape(B * R, W), grad_util, grad_taste


def solution(mesh):
    rows = ("groups", "state")
    return jax.shard_map(
        local,
        mesh=mesh,
        in_specs=(
            P(rows, "type"),
            P(rows, "type"),
            P(None, rows),
            P(None, ("groups", "type")),
            P(rows, None, None, None, None),
            P(rows, None, None),
            P(rows, None),
        ),
        out_specs=(P(rows, "type"), P(rows, "type"), P(None, rows), P(None, ("groups", "type"))),
        check_vma=False,
    )
```

profile of v0, /device:TPU:0, one launch (start us, length us, event | category | flops | bytes accessed | tf_op | source)
XLA Modules:
  0.0 178.8 jit_solution(5393748414620599471)
XLA Ops:
  0.6 3.8 %plan.1 = (s32[4,1,128]{2,1,0:T(1,128)}, s32[192]{0:T(256)}, s32[24]{0:T(128)}) custom-call(s32[1]{0:T(128)} %bitcast.me_ref, s32[6,2,16]{2,1,0:T(2,128)} %bitcast.21, s32[2,16]{1,0:T(2,128)} %bitcast.22), custom_call_target="tpu_custom_call" | custom-call | tf_op jit(solution)/shard_map/plan/pallas_call | solution.py:345
  4.5 8.6 %request.1.want_ref = s32[4,1,128]{2,1,0:T(1,128)} custom-call(s32[4,1,128]{2,1,0:T(1,128)} %get-tuple-element.29.req_ref), custom_call_target="tpu_custom_call" | custom-call | tf_op jit(solution)/shard_map/request/pallas_call | solution.py:354
  13.0 3.7 %gather.1 = (bf16[24,128,256]{2,1,0:T(8,128)(2,1)}, bf16[24,128,256]{2,1,0:T(8,128)(2,1)}) custom-call(s32[4,1,128]{2,1,0:T(1,128)} %request.1.want_ref, bf16[16,128,512]{2,1,0:T(8,128)(2,1)} %bitcast.12), custom_call_target="tpu_custom_call" | custom-call | tf_op jit(solution)/shard_map/gather/pallas_call | solution.py:367
  16.7 67.3 %fetch.1 = (f32[2048,256]{1,0:T(8,128)}, bf16[16,2,128,256]{3,2,1,0:T(8,128)(2,1)}, bf16[24,128,256]{2,1,0:T(8,128)(2,1)}, f32[16,128,2]{2,1,0:T(8,128)}, f32[2,...) custom-call(s32[192]{0:T(256)} %get-tuple-element.27.look_ref, s32[24]{0:T(128)} %get-tuple-element.28.from_ref, ...), custom_call_target="tpu_custom_call" | custom-call | flops 1610612736 | bytes 12582912 | tf_op jit(solution)/shard_map/fetch/pallas_call | solution.py:412
  84.0 11.9 %all-to-all-start.1 = ((bf16[4,6,128,256]{3,2,1,0:T(8,128)(2,1)}), bf16[4,6,128,256]{3,2,1,0:T(8,128)(2,1)S(1)}, u32[]{:S(2)}, u32[]{:S(2)}) async-start(bf16[4,6,128,256]{3,2,1,0:T(8,128)(2,1)} %bitcast.20), calls=%async_computation.1 | async-start | bytes 3145728 | tf_op jit(solution)/shard_map/all_to_all | solution.py:377
  95.9 7.8 %back.3.adj_ref = f32[17,128,256]{2,1,0:T(8,128)} custom-call(s32[192]{0:T(256)} %get-tuple-element.27.look_ref, bf16[16,2,6,128,128]{4,3,2,1,0:T(8,128)(2,1)} %tiles_ref.5, bf16[16,2,128,256]{3,2,1,0:T(8,128)(2,1)} %get-tuple-element.37.scaled_ref), custom_call_target="tpu_custom_call" | custom-call | flops 1610612736 | bytes 7340032 | tf_op jit(solution)/shard_map/back/pallas_call | solution.py:441
  103.7 18.1 %value.1 = (f32[2048,512]{1,0:T(8,128)}, bf16[16,2,128,256]{3,2,1,0:T(8,128)(2,1)}, bf16[24,128,256]{2,1,0:T(8,128)(2,1)}, f32[16,128,2]{2,1,0:T(8,128)}, f32[2,256]{1,0:T(2,128)}) custom-call(s32[192]{0:T(256)} %get-tuple-element.27.look_ref, s32[24]{0:T(128)} %get-tuple-element.28.from_ref, bf16[16,128,512]{2,1,0:T(8,128)(2,1)} %bitcast.14, ...), custom_call_target="tpu_custom_call" | custom-call | flops 1610612736 | bytes 12582912 | tf_op jit(solution)/shard_map/value/pallas_call | solution.py:424
  121.8 9.5 %all-to-all-done.1 = bf16[4,6,128,256]{3,2,1,0:T(8,128)(2,1)S(1)} async-done(((bf16[4,6,128,256]{3,2,1,0:T(8,128)(2,1)}), bf16[4,6,128,256]{3,2,1,0:T(8,128)(2,1)S(1)}, u32[]{:S(2)}, u32[]{:S(2)}) %all-to-all-start.1) | async-done | bytes 1572896 | tf_op jit(solution)/shard_map/all_to_all | solution.py:377
  131.3 0.0 copy-start
  131.3 3.6 %all-to-all-start = ((bf16[4,6,128,256]{3,2,1,0:T(8,128)(2,1)}), bf16[4,6,128,256]{3,2,1,0:T(8,128)(2,1)S(1)}, u32[]{:S(2)}, u32[]{:S(2)}) async-start(bf16[4,6,128,256]{3,2,1,0:T(8,128)(2,1)} %bitcast.19), calls=%async_computation | async-start | bytes 3145728 | tf_op jit(solution)/shard_map/all_to_all | solution.py:377
  134.9 0.0 copy-start.4
  134.9 0.0 copy-start.5
  134.9 2.7 %add_multiply_fusion = f32[16,128,2]{2,1,0:T(8,128)} fusion(f32[16,128,2]{2,1,0:T(8,128)} %get-tuple-element.43, f32[16,128,2]{2,1,0:T(8,128)} %get-tuple-element.44), kind=kLoop, calls=%fused_computation | loop fusion | flops 8192 | bytes 49152 | tf_op jit(solution)/shard_map/div | solution.py:464
  137.7 0.0 copy-done
  137.7 2.2 %copy.13.gu_ref = f32[2,2048]{1,0:T(2,128)} copy(f32[2,2048]{0,1:T(8,128)} %bitcast.17) | data formatting | bytes 32768 | tf_op jit(solution)/shard_map/div | solution.py:464
  139.8 0.0 copy-done.4
  139.8 0.0 copy-done.5
  139.8 0.6 maximum_multiply_fusion.gt_ref
  140.4 7.8 %back.2.adj_ref.after_ref = f32[17,128,256]{2,1,0:T(8,128)} custom-call(s32[192]{0:T(256)} %get-tuple-element.27.look_ref, bf16[16,2,6,128,128]{4,3,2,1,0:T(8,128)(2,1)} %tiles_ref.5, bf16[16,2,128,256]{3,2,1,0:T(8,128)(2,1)} %get-tuple-element.35.scaled_ref), custom_call_target="tpu_custom_call" | custom-call | flops 1610612736 | bytes 7340032 | tf_op jit(solution)/shard_map/back/pallas_call | solution.py:441
  148.2 3.9 %land.2 = (f32[16,128,512]{2,1,0:T(8,128)}, s32[1]{0:T(128)}) custom-call(s32[4,1,128]{2,1,0:T(1,128)} %request.1.want_ref, f32[17,128,256]{2,1,0:T(8,128)} %back.3.adj_ref, bf16[24,128,256]{2,1,0:T(8,128)(2,1)} %bitcast.15), custom_call_target="tpu_custom_call" | custom-call | tf_op jit(solution)/shard_map/land/pallas_call | solution.py:467
  152.2 20.3 %sums.1 = (f32[2,2048]{1,0:T(2,128)}, f32[2,512]{1,0:T(2,128)}) custom-call(f32[2,2048]{1,0:T(2,128)} %copy.13.gu_ref, f32[2,512]{1,0:T(2,128)} %maximum_multiply_fusion.gt_ref, s32[1]{0:T(128)} %get-tuple-element.47.token_ref, f32[17,128,256]{2,1,0:T(8,128)} %back.2.adj_ref.after_ref), custom_call_target="tpu_custom_call" | custom-call | bytes 8388608 | tf_op jit(solution)/shard_map/sums/pallas_call | solution.py:478
  172.5 0.0 all-to-all-done
  172.5 0.0 copy-start.1
  172.5 1.2 copy-done.1
  173.7 0.0 copy-start.2
  173.7 0.0 copy-start.3
  173.7 3.9 %land.3 = (f32[16,128,512]{2,1,0:T(8,128)}, s32[1]{0:T(128)}) custom-call(s32[4,1,128]{2,1,0:T(1,128)} %request.1.want_ref, f32[17,128,256]{2,1,0:T(8,128)} %back.2.adj_ref.after_ref, bf16[24,128,256]{2,1,0:T(8,128)(2,1)} %bitcast.16, f32[16,128,512]{2,1,0:T(8,128)} %get-tuple-element.41.rest_0_), custom_call_target="tpu_custom_call", output_to_operand_aliasing={{0}: (3, {})} | custom-call | tf_op jit(solution)/shard_map/land/pallas_call | solution.py:467
  177.6 0.0 copy-done.2
  177.6 0.6 copy.17
  178.2 0.0 copy-done.3
  178.2 0.6 copy.18
Async XLA Ops:
  84.0 47.3 %all-to-all-start.1 = ((bf16[4,6,128,256]{3,2,1,0:T(8,128)(2,1)}), bf16[4,6,128,256]{3,2,1,0:T(8,128)(2,1)S(1)}, u32[]{:S(2)}, u32[]{:S(2)}) async-start(bf16[4,6,128,256]{3,2,1,0:T(8,128)(2,1)} %bitcast.20), calls=%async_computation.1 | async-start | bytes 3145728 | tf_op jit(solution)/shard_map/all_to_all | solution.py:377
  131.3 6.3 %copy-start = (bf16[4,6,128,256]{3,2,1,0:T(8,128)(2,1)}, bf16[4,6,128,256]{3,2,1,0:T(8,128)(2,1)S(1)}, u32[]{:S(2)}) copy-start(bf16[4,6,128,256]{3,2,1,0:T(8,128)(2,1)S(1)} %all-to-all-done.1) | copy-start | bytes 4718596
  131.3 41.1 %all-to-all-start = ((bf16[4,6,128,256]{3,2,1,0:T(8,128)(2,1)}), bf16[4,6,128,256]{3,2,1,0:T(8,128)(2,1)S(1)}, u32[]{:S(2)}, u32[]{:S(2)}) async-start(bf16[4,6,128,256]{3,2,1,0:T(8,128)(2,1)} %bitcast.19), calls=%async_computation | async-start | bytes 3145728 | tf_op jit(solution)/shard_map/all_to_all | solution.py:377
  134.9 4.9 %copy-start.4 = (f32[2,256]{1,0:T(2,128)S(1)}, f32[2,256]{1,0:T(2,128)}, u32[]{:S(2)}) copy-start(f32[2,256]{1,0:T(2,128)} %get-tuple-element.45) | copy-start | bytes 6148
  134.9 4.9 %copy-start.5 = (f32[2,256]{1,0:T(2,128)S(1)}, f32[2,256]{1,0:T(2,128)}, u32[]{:S(2)}) copy-start(f32[2,256]{1,0:T(2,128)} %get-tuple-element.46) | copy-start | bytes 6148
  172.5 1.2 copy-start.1
  173.7 3.9 %copy-start.2 = (f32[2,2048]{1,0:T(2,128)S(1)}, f32[2,2048]{1,0:T(2,128)}, u32[]{:S(2)}) copy-start(f32[2,2048]{1,0:T(2,128)} %get-tuple-element.56) | copy-start | bytes 49156
  173.7 4.6 %copy-start.3 = (f32[2,512]{1,0:T(2,128)S(1)}, f32[2,512]{1,0:T(2,128)}, u32[]{:S(2)}) copy-start(f32[2,512]{1,0:T(2,128)} %get-tuple-element.57) | copy-start | bytes 12292
where the time goes:
time: 179 us
  Pallas kernels  145 us (81%)
  starting transfers between devices  15.4 us (9%)
  waiting for transfers between devices  9.51 us (5%)
  local copies, waits for them, and re-layouts  4.55 us (3%)
  other arithmetic  3.34 us (2%)
    pallas_call x1, Pallas kernels, local(): pl.pallas_call(functools.partial(fetch_value_kernel, G, 32, D), grid=(B /...  67.3 us
    pallas_call x1, Pallas kernels, local(): pl.pallas_call(functools.partial(sums_kernel, D, T), out_shape=(shape((A,...  20.3 us
    pallas_call x1, Pallas kernels, local(): pl.pallas_call(functools.partial(value_kernel, G, 32, h * V), grid=(B //...  18.1 us
    pallas_call x2, Pallas kernels, local(): pl.pallas_call(functools.partial(back_kernel, G, A, M), grid=(B // G,), o...  15.6 us
    all_to_all x2, starting transfers between devices, exchange(): lax.all_to_all(x.reshape(D, cap, R, V), 'state', split_axis=0, concat_axi...  15.4 us
    all_to_all x2, waiting for transfers between devices, exchange(): lax.all_to_all(x.reshape(D, cap, R, V), 'state', split_axis=0, concat_axi...  9.51 us
    pallas_call x1, Pallas kernels, local(): pl.pallas_call(functools.partial(request_kernel, D), out_shape=shape((D,...  8.55 us
    pallas_call x2, Pallas kernels, local(): pl.pallas_call(functools.partial(land_kernel, D, cap), grid=(1,), out_sha...  7.84 us
  transfers between devices with their start and end apart: 2, of which 1 were waited for; matrix products, arithmetic and copies ran while one was open for 3% of the time, Pallas kernels for 32%

commit v1 on v0

--- a/solution.py
+++ b/solution.py
@@ -493,10 +493,544 @@
     return value, adjoint.reshape(B * R, W), grad_util, grad_taste
 
 
+def meet_kernel(dims, dest_ref, count_ref, plan_ref, send_ref, mine, land, oh, ssem, rsem):
+    B, A, M, D, cap, Q = dims
+    f32 = jnp.float32
+    y, z = lax.axis_index("groups"), lax.axis_index("state")
+    q = y * D + z
+    E2 = oh.shape[0]
+    mine[...] = jnp.full(mine.shape, -1.0, f32)
+    for n in range(M):
+        mine[n * A : (n + 1) * A, 0:B] = jnp.where(n < count_ref[...], dest_ref[n], -1).astype(f32)
+    land[0] = jnp.transpose(mine[...])[0:B, :]
+
+    def member(k):
+        p = lax.rem(q + k, Q)
+        return {"groups": lax.div(p, D), "state": lax.rem(p, D)}
+
+    greet("state", [member(k) for k in range(1, Q)])
+    copies = [
+        pltpu.make_async_remote_copy(
+            src_ref=land.at[0], dst_ref=land.at[k], send_sem=ssem.at[k], recv_sem=rsem.at[k],
+            device_id=member(k), device_id_type=MESH,
+        )
+        for k in range(1, Q)
+    ]
+    for c in copies:
+        c.start()
+
+    lane = lax.broadcasted_iota(jnp.int32, (B, 128), 1).astype(f32)
+    oh[...] = jnp.zeros(oh.shape, f32)
+    own = land[0]
+    for c in range(A * M):
+        oh[c * B : (c + 1) * B, :] = jnp.where(own[:, c : c + 1] == lane, 1.0, 0.0)
+    for c in copies:
+        c.wait()
+
+    def need_of(table):
+        total = jnp.zeros((B, 128), f32)
+        for c in range(A * M):
+            total = jnp.maximum(total, jnp.where(table[:, c : c + 1] == lane, 1.0, 0.0))
+        return jnp.max(total, axis=0, keepdims=True)
+
+    seg = lax.div(lax.broadcasted_iota(jnp.int32, (1, 128), 1), B)
+    b = lax.broadcasted_iota(jnp.int32, (1, 128), 1).astype(f32)
+    half = D // 2
+    rows, needs = [], []
+    for u in range(Q // D):
+        g = lax.rem(y + u, Q // D)
+        need = [need_of(land[lax.rem(q - (g * D + r) + Q, Q)]) for r in range(D)]
+        end = jnp.where(seg < half, need[D - 1], need[0])
+        gate = jnp.where(seg < half, need[half], need[half - 1]) * (1.0 - end)
+        rows += [end, gate]
+        if u == 0:
+            needs = need
+    peer = 2 * lax.div(z, 2) + 1 - lax.rem(z, 2)
+    mine_need = sum(jnp.where(z == r, needs[r], 0.0) for r in range(D))
+    peer_need = sum(jnp.where(peer == r, needs[r], 0.0) for r in range(D))
+    at = len(rows)
+    rows += [mine_need, peer_need]
+    stack = jnp.concatenate(rows + [jnp.zeros((8 - len(rows), 128), f32)], axis=0)
+    one = lax.broadcasted_iota(jnp.int32, (128, 128), 0)
+    two = lax.broadcasted_iota(jnp.int32, (128, 128), 1)
+    same = jnp.where(lax.div(one, B) == lax.div(two, B), 1.0, 0.0)
+    below = jnp.where(one < two, same, 0.0)
+    rank = jnp.dot(stack, below, preferred_element_type=f32)
+    size = jnp.dot(stack, same, preferred_element_type=f32)
+    far_any = rows[0] + rows[1]
+    far_rank = jnp.where(rows[0] > 0, rank[0:1], size[0:1] + rank[1:2])
+    most = size[0:1] + size[1:2]
+    for u in range(1, Q // D):
+        most = jnp.maximum(most, size[2 * u : 2 * u + 1] + size[2 * u + 1 : 2 * u + 2])
+    near_rank, give_rank = rank[at : at + 1], rank[at + 1 : at + 2]
+    first = (z * B).astype(f32)
+    FX = 2 * cap
+    row_of = 1.0 + jnp.where(
+        seg == z,
+        b - first,
+        jnp.where(
+            lax.div(seg, 2) == lax.div(z, 2), B + near_rank, B + cap + lax.rem(seg, 2).astype(f32) * FX + far_rank
+        ),
+    )
+
+    def as_row(col):
+        full = jnp.broadcast_to(col, (E2, 128))
+        return jnp.concatenate(
+            [jnp.transpose(full[k : k + 128, :])[0:1, :] for k in range(0, E2, 128)], axis=1
+        )
+
+    row = jnp.sum(oh[...] * row_of, axis=1, keepdims=True)
+    key = jnp.where(row == 0, 200.0, jnp.where(row > B, row, row + 100.0))
+    iq = lax.broadcasted_iota(jnp.int32, (E2, 1), 0)
+    order = key * E2 + iq.astype(f32)
+    order_row, key_row = as_row(order), as_row(key)
+    pos = jnp.sum(jnp.where(order_row < order, 1.0, 0.0), axis=1, keepdims=True)
+    less = jnp.sum(jnp.where(key_row < key, 1.0, 0.0), axis=1, keepdims=True)
+    wide = lax.broadcasted_iota(jnp.int32, (E2, E2), 1).astype(f32)
+    c = lax.div(iq, B)
+    entry = ((lax.rem(iq, B) * A + lax.rem(c, A)) * M + lax.div(c, A)).astype(f32)
+    move = jnp.where(pos == wide, 1.0, 0.0)
+    sort_row = jnp.sum(move * entry, axis=0, keepdims=True)
+    prev_row = jnp.sum(move * jnp.where(pos == less, 0.0, pos), axis=0, keepdims=True)
+    look_row = jnp.sum(jnp.where(entry == wide, row, 0.0), axis=0, keepdims=True)
+    row_key = jnp.where(b >= B, b + 1.0, b + 101.0)
+    last = jnp.sum(jnp.where(key <= row_key, 1.0, 0.0), axis=0, keepdims=True)
+    used = jnp.max(jnp.where(key == row_key, 1.0, 0.0), axis=0, keepdims=True)
+    put = lambda k, v: plan_ref.__setitem__((slice(k, k + 1), slice(0, v.shape[1])), v.astype(jnp.int32))
+    plan_ref[...] = jnp.zeros(plan_ref.shape, jnp.int32)
+    put(0, look_row)
+    put(1, sort_row)
+    put(2, prev_row)
+    put(3, last * used)
+    put(4, jnp.where((peer_need > 0) & (seg == z), give_rank + 1.0, 0.0))
+    put(5, jnp.where((far_any > 0) & (seg == z), far_rank + 1.0, 0.0))
+    put(6, jnp.broadcast_to(jnp.max(most, axis=1, keepdims=True), (1, 128)))
+    slot = lax.broadcasted_iota(jnp.int32, (16, 128), 0).astype(f32)
+    here = jnp.where(seg == z, b - first, 0.0)
+    near = jnp.sum(
+        jnp.where(give_rank == slot, jnp.where(peer_need > 0, here, 0.0), 0.0), axis=1, keepdims=True
+    )
+    far = jnp.sum(jnp.where(far_rank == slot, jnp.where(far_any > 0, here, 0.0), 0.0), axis=1, keepdims=True)
+    send_ref[0:16, :] = jnp.broadcast_to(near, (16, 128)).astype(jnp.int32)
+    send_ref[16:32, :] = jnp.broadcast_to(far, (16, 128)).astype(jnp.int32)
+
+
+def sweep_kernel(dims, plan, send, val, cot_hbm, tiles_hbm, util, taste, value_hbm, adj_hbm, gu_ref, gt_ref, *rest):
+    B, A, M, R, V, H, D, T, cap, FX, F, G, rows = dims
+    f32, bf16 = jnp.float32, jnp.bfloat16
+    E, C, CH = B * A * M, cap // 2, 2
+    tables, retn, retf, rest = rest[:H], rest[H : 2 * H], rest[2 * H : 3 * H], rest[3 * H :]
+    (own, stn, stx, tiles, cot, vout, scaled, P, bst, rel, adj, acc, fold, gacc, gtac, lu, lt,
+     lsem, vsem, asem, sn, rn, sx, rx, sf, bsn, brn, bsx, brel, brx, usem, ursem, tsem, trsem) = rest
+    z, t = lax.axis_index("state"), lax.axis_index("type")
+    side = lax.div(z, 2)
+    spot = lax.rem(z, 2)
+    peer = 2 * side + 1 - spot
+    gate_to = D // 2 - side
+    is_gate = (z == D // 2 - 1) | (z == D // 2)
+    is_end = jnp.logical_not(is_gate)
+    far0 = 2 * (1 - side)
+    tail = [C] if F > cap else []
+
+    def span(c):
+        return pl.ds(cap, F - cap) if isinstance(c, int) and c == C else pl.ds(c * CH, CH)
+
+    def remote(src, dst, s, r, device):
+        return pltpu.make_async_remote_copy(
+            src_ref=src, dst_ref=dst, send_sem=s, recv_sem=r, device_id={"state": device}, device_id_type=MESH
+        )
+
+    def shift(c, base):
+        s = span(c)
+        return pl.ds(base + s.start, s.size)
+
+    def fwd_near(h):
+        return remote(stn.at[h], tables[h].at[pl.ds(B, cap)], sn.at[h], rn.at[h], peer)
+
+    def fwd_far(h, c, x):
+        return remote(
+            stx.at[h, span(c)], tables[h].at[shift(c, B + cap + x * FX)], sx.at[h, c], rx.at[h, x, c], gate_to
+        )
+
+    def fwd_pass(h, x, c):
+        part = tables[h].at[shift(c, B + cap + x * FX)]
+        return remote(part, part, sf.at[h, x, c], rx.at[h, x, c], peer)
+
+    def bwd_near(h):
+        return remote(bst.at[h, pl.ds(0, cap)], retn[h], bsn.at[h], brn.at[h], peer)
+
+    def bwd_far(h, x, c):
+        return remote(
+            bst.at[h, shift(c, cap + x * FX)], retf[h].at[span(c)], bsx.at[h, x, c], brx.at[h, c], far0 + x
+        )
+
+    def bwd_end(h, x, c):
+        return remote(
+            bst.at[h, shift(c, cap + x * FX)], rel.at[h, x, span(c)], bsx.at[h, x, c], brel.at[h, x, c], peer
+        )
+
+    def cols(h):
+        return pl.ds(h * V, V)
+
+    own_copy = pltpu.make_async_copy(val, own, lsem.at[0])
+    own_copy.start()
+    fills = [
+        pltpu.make_async_copy(val.at[:, :, cols(h)], tables[h].at[pl.ds(0, B)], lsem.at[1 + h]) for h in range(H)
+    ]
+    fills[0].start()
+    tile_copy = pltpu.make_async_copy(tiles_hbm, tiles, lsem.at[1 + H])
+    cot_copy = pltpu.make_async_copy(cot_hbm, cot, lsem.at[2 + H])
+    greet(
+        "state",
+        [{"state": lax.rem(z + k, D)} for k in range(1, D)] + [{"type": lax.rem(t + k, T)} for k in range(1, T)],
+    )
+    own_copy.wait()
+    for h in range(H):
+        for s in range(F):
+            stx[h, s] = own[send[16 + s, 0], :, h * V : (h + 1) * V]
+            if s >= 2 and s % CH == 1 and s - CH < cap:
+                fwd_far(h, s // CH - 1, spot).start()
+        for s in range(cap):
+            stn[h, s] = own[send[s, 0], :, h * V : (h + 1) * V]
+        if F <= cap + 1:
+            fwd_far(h, C - 1, spot).start()
+        for c in tail:
+            fwd_far(h, c, spot).start()
+        fwd_near(h).start()
+        if h == 0:
+            tile_copy.start()
+            cot_copy.start()
+            for f in fills[1:]:
+                f.start()
+    P[0] = jnp.zeros((R, V), f32)
+    gtac[...] = jnp.zeros(gtac.shape, f32)
+
+    def pass_on(h, c):
+        @pl.when(is_gate)
+        def _():
+            for x in range(2):
+                fwd_far(h, c, x).wait_recv()
+                fwd_pass(h, x, c).start()
+
+    def arrived(h):
+        fwd_near(h).wait_recv()
+
+        @pl.when(is_gate)
+        def _():
+            for x in range(2):
+                for c in tail:
+                    fwd_far(h, c, x).wait_recv()
+
+        @pl.when(is_end)
+        def _():
+            for x in range(2):
+                for c in range(C):
+                    fwd_far(h, c, x).wait_recv()
+
+    def values(h, hook):
+        t0, t1 = taste[0:1, h * V : (h + 1) * V], taste[1:2, h * V : (h + 1) * V]
+
+        def step(k, carry):
+            for g in range(G):
+                i = k * G + g
+                for a in range(A):
+                    weights, blocks = [], []
+                    for n in range(M):
+                        e = (i * A + a) * M + n
+                        row = plan[0, e]
+                        keep = jnp.where(row > 0, 1.0, 0.0).astype(f32)
+                        tile = tiles[e]
+                        weights.append(tile * jnp.full(tile.shape, keep, f32).astype(bf16))
+                        blocks.append(tables[h][jnp.maximum(row - 1, 0)])
+                    acc[g, a] = jnp.dot(
+                        jnp.concatenate(weights, axis=1), jnp.concatenate(blocks, axis=0),
+                        preferred_element_type=f32,
+                    )
+            for g in range(G):
+                i = k * G + g
+                lanes = pl.ds(pl.multiple_of(i * R, R), R)
+                base = [jnp.transpose(jnp.broadcast_to(util[a : a + 1, lanes], (R, R))) for a in range(A)]
+                g0 = g1 = 0.0
+                for c in range(0, R, rows):
+                    at = slice(c, c + rows)
+                    here = pl.ds(pl.multiple_of(i * R + c, rows), rows)
+                    q0 = base[0][at, 0:1] + t0 + 0.95 * acc[g, 0, at, :]
+                    q1 = base[1][at, 0:1] + t1 + 0.95 * acc[g, 1, at, :]
+                    gap = q1 - q0
+                    small = jnp.exp(-jnp.abs(gap))
+                    total = 1.0 + small
+                    vout[here, :] = jnp.maximum(q0, q1) + jnp.log(total)
+                    big = cot[here, h * V : (h + 1) * V].astype(f32) / total
+                    little = big * small
+                    first_wins = gap <= 0.0
+                    h0 = jnp.where(first_wins, big, little)
+                    h1 = jnp.where(first_wins, little, big)
+                    scaled[i * A, at, :] = (0.95 * h0).astype(bf16)
+                    scaled[i * A + 1, at, :] = (0.95 * h1).astype(bf16)
+                    fold[0, at, :] = sum(h0[:, w : w + 128] for w in range(0, V, 128))
+                    fold[1, at, :] = sum(h1[:, w : w + 128] for w in range(0, V, 128))
+                    g0, g1 = g0 + h0, g1 + h1
+                for a in range(A):
+                    line = jnp.sum(jnp.transpose(fold[a]), axis=0, keepdims=True)
+                    gacc[a : a + 1, lanes] = line if h == 0 else gacc[a : a + 1, lanes] + line
+                gtac[0:1, h * V : (h + 1) * V] += jnp.sum(g0, axis=0, keepdims=True)
+                gtac[1:2, h * V : (h + 1) * V] += jnp.sum(g1, axis=0, keepdims=True)
+            part = pl.ds(k * G * R, G * R)
+            pltpu.make_async_copy(vout.at[part], value_hbm.at[part, cols(h)], vsem.at[k]).start()
+            hook(k)
+            return carry
+
+        lax.fori_loop(0, B // G, step, 0)
+
+    def value_done(h):
+        for k in range(B // G):
+            part = pl.ds(k * G * R, G * R)
+            pltpu.make_async_copy(vout.at[part], value_hbm.at[part, cols(h)], vsem.at[k]).wait()
+
+    def back(lo, hi):
+        def step(k, carry):
+            for u in range(B):
+                e = plan[1, k * B + u]
+                P[k * B + u + 1] = P[plan[2, k * B + u]] + transposed_dot(tiles[e], scaled[lax.div(e, M)])
+            return carry
+
+        lax.fori_loop(lo, hi, step, 0)
+
+    def stage(h, s):
+        bst[h, s] = P[plan[3, B + s]].astype(bf16)
+
+    def give(h):
+        @pl.when(is_end)
+        def _():
+            for c in range(C):
+                for x in range(2):
+                    for s in range(c * CH, (c + 1) * CH):
+                        stage(h, cap + x * FX + s)
+                if c > 0:
+                    for x in range(2):
+                        bwd_end(h, x, c - 1).start()
+
+        @pl.when(is_gate)
+        def _():
+            for x in range(2):
+                for s in range(cap, F):
+                    stage(h, cap + x * FX + s)
+
+        for s in range(cap):
+            stage(h, s)
+
+        @pl.when(is_end)
+        def _():
+            for x in range(2):
+                bwd_end(h, x, C - 1).start()
+
+        @pl.when(is_gate)
+        def _():
+            for x in range(2):
+                for c in tail:
+                    bwd_far(h, x, c).start()
+
+        bwd_near(h).start()
+
+    def add_on(h, c):
+        @pl.when(is_gate)
+        def _():
+            for x in range(2):
+                bwd_end(h, x, c).wait_recv()
+                for s in range(CH):
+                    u = c * CH + s
+                    term = P[plan[3, B + cap + x * FX + u]] + rel[h, x, u].astype(f32)
+                    bst[h, cap + x * FX + u] = term.astype(bf16)
+            for x in range(2):
+                bwd_far(h, x, c).start()
+
+    def keep(h):
+        def step(j, carry):
+            adj[h, j] = P[plan[3, j]]
+            return carry
+
+        lax.fori_loop(0, B, step, 0)
+
+    def adj_out(h, k):
+        part = pl.ds(k * G, G)
+        return pltpu.make_async_copy(adj.at[h, part], adj_hbm.at[part, :, cols(h)], asem.at[h, k])
+
+    def land(h):
+        bwd_near(h).wait_recv()
+        for c in list(range(C)) + tail:
+            bwd_far(h, 0, c).wait_recv()
+
+        def step(k, carry):
+            for g in range(G):
+                j = k * G + g
+                near, far = plan[4, z * B + j], plan[5, z * B + j]
+                add = jnp.where(near > 0, retn[h][jnp.maximum(near - 1, 0)].astype(f32), 0.0)
+                add += jnp.where(far > 0, retf[h][jnp.maximum(far - 1, 0)].astype(f32), 0.0)
+                adj[h, j] = (adj[h, j] if h < H - 1 else P[plan[3, j]]) + add
+            adj_out(h, k).start()
+            return carry
+
+        lax.fori_loop(0, B // G, step, 0)
+
+    def sums():
+        out = []
+        for k in range(1, T):
+            out.append(
+                pltpu.make_async_remote_copy(
+                    src_ref=gacc, dst_ref=lu.at[k], send_sem=usem.at[k], recv_sem=ursem.at[k],
+                    device_id={"type": lax.rem(t + k, T)}, device_id_type=MESH,
+                )
+            )
+        for k in range(1, D):
+            out.append(remote(gtac, lt.at[k], tsem.at[k], trsem.at[k], lax.rem(z + k, D)))
+        return out
+
+    for c in range(C):
+        pass_on(0, c)
+    fills[0].wait()
+    arrived(0)
+    tile_copy.wait()
+    cot_copy.wait()
+    for h in range(H):
+        steps = B // G
+
+        def hook(k, h=h):
+            @pl.when(k < C)
+            def _():
+                if h + 1 < H:
+                    pass_on(h + 1, k)
+                if h > 0:
+                    add_on(h - 1, k)
+
+        if h > 0:
+            fills[h].wait()
+            arrived(h)
+            value_done(h - 1)
+        values(h, hook)
+        back(0, 1)
+        give(h)
+        if h == H - 1:
+            for c in sums():
+                c.start()
+        back(1, E // B)
+        if h < H - 1:
+            keep(h)
+        if h > 0:
+            land(h - 1)
+    for c in range(C):
+        add_on(H - 1, c)
+    for c in sums():
+        c.wait()
+    lu[0] = gacc[...]
+    lt[0] = gtac[...]
+    u = lu[lax.rem(t, T)]
+    for j in range(1, T):
+        u = u + lu[lax.rem(t - j + T, T)]
+    w = lt[lax.rem(z, D)]
+    for j in range(1, D):
+        w = w + lt[lax.rem(z - j + D, D)]
+    gu_ref[...] = u / (H * V * T)
+    gt_ref[...] = w / (B * R * D)
+    land(H - 1)
+    value_done(H - 1)
+    for h in range(H):
+        for k in range(B // G):
+            adj_out(h, k).wait()
+        fwd_near(h).wait_send()
+        bwd_near(h).wait_send()
+        for c in list(range(C)) + tail:
+            fwd_far(h, c, spot).wait_send()
+
+        @pl.when(is_gate)
+        def _(h=h):
+            for x in range(2):
+                for c in range(C):
+                    fwd_pass(h, x, c).wait_send()
+                for c in list(range(C)) + tail:
+                    bwd_far(h, x, c).wait_send()
+
+        @pl.when(is_end)
+        def _(h=h):
+            for x in range(2):
+                for c in range(C):
+                    bwd_end(h, x, c).wait_send()
+
+
+def folded(value_in, cotangent, state_util, taste, tiles, dest_block, counts):
+    B, A, M, R, _ = tiles.shape
+    W = value_in.shape[1]
+    D, T = lax.axis_size("state"), lax.axis_size("type")
+    Q = lax.axis_size("groups") * D
+    cap = (B + D - 2) // (D - 1)
+    E, FX, H, G = B * A * M, 2 * cap, 2, 4
+    V = W // H
+    f32, bf16, i32 = jnp.float32, jnp.bfloat16, jnp.int32
+    shape, DMA = jax.ShapeDtypeStruct, pltpu.SemaphoreType.DMA
+    vmem = pl.BlockSpec(memory_space=VMEM)
+    hbm = pl.BlockSpec(memory_space=pl.ANY)
+
+    plan, send = pl.pallas_call(
+        functools.partial(meet_kernel, (B, A, M, D, cap, Q)),
+        out_shape=(shape((8, 256), i32), shape((32, 128), i32)),
+        in_specs=[vmem] * 2,
+        out_specs=[vmem] * 2,
+        scratch_shapes=[VMEM((128, 128), f32), VMEM((Q, B, 128), f32), VMEM((256, 128), f32), DMA((Q,)), DMA((Q,))],
+        compiler_params=pltpu.CompilerParams(collective_id=0, has_side_effects=True),
+        name="meet",
+    )(dest_block.transpose(2, 1, 0), counts.T)
+
+    def sweep(F, ident):
+        dims = (B, A, M, R, V, H, D, T, cap, FX, F, G, 32)
+        C = cap // 2
+        return pl.pallas_call(
+            functools.partial(sweep_kernel, dims),
+            out_shape=(
+                shape((B * R, W), f32), shape((B, R, W), f32), shape((A, B * R), f32), shape((A, W), f32),
+            ),
+            in_specs=[smem(), smem(), hbm, hbm, hbm, vmem, vmem],
+            out_specs=[hbm, hbm, vmem, vmem],
+            scratch_shapes=[VMEM((B + cap + 2 * FX, R, V), bf16)] * H
+            + [VMEM((cap, R, V), bf16)] * H
+            + [VMEM((FX, R, V), bf16)] * H
+            + [
+                VMEM((B, R, W), bf16), VMEM((H, cap, R, V), bf16), VMEM((H, FX, R, V), bf16),
+                VMEM((E, R, R), bf16), VMEM((B * R, W), bf16), VMEM((B * R, V), f32),
+                VMEM((B * A, R, V), bf16), VMEM((E + 1, R, V), f32), VMEM((H, cap + 2 * FX, R, V), bf16),
+                VMEM((H, 2, cap, R, V), bf16), VMEM((H, B, R, V), f32), VMEM((G, A, R, V), f32),
+                VMEM((A, R, 128), f32), VMEM((A, B * R), f32), VMEM((A, W), f32),
+                VMEM((T, A, B * R), f32), VMEM((D, A, W), f32),
+                DMA((3 + H,)), DMA((B // G,)), DMA((H, B // G)), DMA((H,)), DMA((H,)),
+                DMA((H, C + 1)), DMA((H, 2, C + 1)), DMA((H, 2, C)), DMA((H,)), DMA((H,)),
+                DMA((H, 2, C + 1)), DMA((H, 2, C)), DMA((H, C + 1)),
+                DMA((T,)), DMA((T,)), DMA((D,)), DMA((D,)),
+            ],
+            compiler_params=pltpu.CompilerParams(
+                collective_id=ident, has_side_effects=True, vmem_limit_bytes=66_000_000
+            ),
+            cost_estimate=pl.CostEstimate(flops=4 * E * R * R * W, bytes_accessed=20 << 20, transcendentals=3 * B * R * W),
+            name="sweep",
+        )
+
+    value, adjoint, grad_util, grad_taste = sweep(FX, 1)(
+        plan, send, value_in.reshape(B, R, W), cotangent, tiles.reshape(E, R, R), state_util, taste
+    )
+    return value, adjoint.reshape(B * R, W), grad_util, grad_taste
+
+
+def choose(*args):
+    B, A, M, R, _ = args[4].shape
+    D = lax.axis_size("state")
+    cap = (B + D - 2) // (D - 1)
+    fits = D * B <= 128 and 128 < B * A * M <= 256 and cap % 2 == 0 and B % 4 == 0 and R == 128
+    if D == 4 and fits and args[0].shape[1] % 256 == 0:
+        return folded(*args)
+    return local(*args)
+
+
 def solution(mesh):
     rows = ("groups", "state")
     return jax.shard_map(
-        local,
+        choose,
         mesh=mesh,
         in_specs=(
             P(rows, "type"),

time: 179 us -> 162 us (0.905)
  starting transfers between devices: 15.4 us -> 0 us
  waiting for transfers between devices: 9.51 us -> 0 us
  Pallas kernels: 145 us -> 153 us
  local copies, waits for them, and re-layouts: 4.55 us -> 8.04 us
  other arithmetic: 3.34 us -> 0 us
    all_to_all x2 -> x0, starting transfers between devices: 15.4 us -> none  [exchange(): lax.all_to_all(x.reshape(D, cap, R, V), 'state', split_axis=0, concat_axi...]
    all_to_all x2 -> x0, waiting for transfers between devices: 9.51 us -> none  [exchange(): lax.all_to_all(x.reshape(D, cap, R, V), 'state', split_axis=0, concat_axi...]
    pallas_call x10 -> x2, Pallas kernels: 145 us -> 153 us  [the longest x1 142 us: folded(): sweep(FX, 1)]
    unnamed x14 -> x10, local copies, waits for them, and re-layouts: 2.39 us -> 8.04 us
    div x2 -> x0, other arithmetic: 3.34 us -> none  [the longest x1 2.75 us: local(): gu_rows = sum(gus).transpose(2, 0, 1).reshape(A, B * R) / (W * T)]
    div x1 -> x0, local copies, waits for them, and re-layouts: 2.16 us -> none  [local(): gu_rows = sum(gus).transpose(2, 0, 1).reshape(A, B * R) / (W * T)]
  transfers between devices with their start and end apart: 2 -> 0, of which waited for: 1 -> 0; matrix products, arithmetic and copies ran while one was open for 3% -> 0% of each run, Pallas kernels for 32% -> 0%
where the time goes in v1:
time: 162 us
  Pallas kernels  153 us (94%)
  local copies, waits for them, and re-layouts  8.04 us (5%)
    pallas_call x1, Pallas kernels, folded(): sweep(FX, 1)  142 us
    pallas_call x1, Pallas kernels, folded(): pl.pallas_call(functools.partial(meet_kernel, (B, A, M, D, cap, Q)), out_...  11.2 us
    unnamed x10, local copies, waits for them, and re-layouts  8.04 us

profile of v1, /device:TPU:0, one launch (start us, length us, event | category | flops | bytes accessed | tf_op | source)
XLA Modules:
  0.0 162.0 jit_solution(12729240940446973519)
XLA Ops:
  0.6 11.2 %meet.1 = (s32[8,256]{1,0:T(8,128)}, s32[32,128]{1,0:T(8,128)}) custom-call(s32[6,2,16]{2,1,0:T(2,128)} %bitcast.6, s32[2,16]{1,0:T(2,128)} %bitcast.7), custom_call_target="tpu_custom_call" | custom-call | tf_op jit(solution)/shard_map/meet/pallas_call | solution.py:972
  11.8 142.1 %sweep.1 = (f32[2048,512]{1,0:T(8,128)}, f32[16,128,512]{2,1,0:T(8,128)}, f32[2,2048]{1,0:T(2,128)}, f32[2,512]{1,0:T(2,128)}) custom-call(s32[8,256]{1,0:T(8,128)} %get-tuple-element.10.plan, s32[32,128]{1,0:T(8,128)} %get-tuple-element.11.send, bf16[16,128,512]{2,1,0:T(8,128)(2,1)} %bitcast.9, bf16[2048,512]{1,0:T(8,128)(2,1)} %cot_hbm.1, ...), custom_call_target="tpu_custom_call" | custom-call | flops 6442450944 | bytes 20971520 | tf_op jit(solution)/shard_map/sweep/pallas_call | solution.py:1014
  154.0 0.0 copy-start
  154.0 4.8 %copy.15 = f32[2048,512]{1,0:T(8,128)} copy(f32[2048,512]{1,0:T(8,128)} %get-tuple-element.20) | data formatting | bytes 8388608
  158.8 0.0 copy-done
  158.8 0.0 copy-start.1
  158.8 0.0 copy-start.2
  158.8 2.0 %copy.16 = f32[2048,512]{1,0:T(8,128)} copy(f32[2048,512]{1,0:T(8,128)S(1)} %bitcast.5) | data formatting | bytes 8388608
  160.8 0.0 copy-done.1
  160.8 0.6 copy.17
  161.4 0.0 copy-done.2
  161.4 0.6 copy.18
Async XLA Ops:
  154.0 4.8 %copy-start = (f32[16,128,512]{2,1,0:T(8,128)S(1)}, f32[16,128,512]{2,1,0:T(8,128)}, u32[]{:S(2)}) copy-start(f32[16,128,512]{2,1,0:T(8,128)} %get-tuple-element.13) | copy-start | bytes 12582916
  158.8 2.0 %copy-start.1 = (f32[2,2048]{1,0:T(2,128)S(1)}, f32[2,2048]{1,0:T(2,128)}, u32[]{:S(2)}) copy-start(f32[2,2048]{1,0:T(2,128)} %get-tuple-element.22) | copy-start | bytes 49156
  158.8 2.6 %copy-start.2 = (f32[2,512]{1,0:T(2,128)S(1)}, f32[2,512]{1,0:T(2,128)}, u32[]{:S(2)}) copy-start(f32[2,512]{1,0:T(2,128)} %get-tuple-element.23) | copy-start | bytes 12292
